TPU v7x, 32 devices: a whole 2x2x4 slice. The times are simulated.
32 devices in a mesh: band: 4 (over y, core), ga: 8 (over z, x).
Axes of the slice: x: 2, y: 2, z: 4, core: 2. Of those that a mesh axis runs over, the one named last changes fastest.
Arguments:
- density: float32 [160, 160, 160], P('ga'), may hold values from -6 to 6
- stick_column: int32 [20480], replicated, may hold values from 0 to 25599, as said below
- vloc: float32 [2, 160, 20480], P(None, None, 'ga'), may hold values from -0.0034179688 to 0.0034179688
- positions: float32 [3, 32], replicated, may hold values from 0 to 1
- species: int32 [32], replicated, may hold values from 0 to 1
- psi: bfloat16 [270336, 2, 1024], P('ga', None, 'band'), may hold values from -6 to 6
- miller_wave: int32 [3, 270336], P(None, 'ga'), may hold values from -40 to 40
- proj_radial: float32 [2, 8, 270336], P(None, None, 'ga'), may hold values from -0.01171875 to 0.01171875
- proj_count: int32 [2], replicated, may hold values from 4 to 8
- dcoef: float32 [2, 8, 8], replicated, may hold values from -0.0625 to 0.0625
- occupation: float32 [1024], P('band'), may hold values from 0 to 2
Outputs:
- density_sticks: float32 [2, 160, 20480], P(None, None, 'ga')
- forces: float32 [3, 32], replicated
Inputs may be any that keep to these rules, and one draw needn't show every extreme that they name: `stick_column`: distinct columns of the 160 by 160 frequency plane.
All inputs are finite; a program needn't handle non-finite values.
Results may differ from a plain program's by a relative error of at most 0.0036.
Values sent between devices are 32-bit elements; how exact they have to be, the bound alone decides.
A program may use at most 192 MiB of HBM per device.

v0:
```python
import math
import jax
import jax.numpy as jnp
from jax import lax
from jax.sharding import PartitionSpec as P

NX = 160
NY = 160
NZ = 160
TWO_PI = 2.0 * math.pi
EXACT = lax.Precision.HIGHEST
FINE = lax.Precision.HIGH


def frequency(index, count):
    return jnp.where(index >= count // 2, index - count, index)


def dft_table(count):
    index = jnp.arange(count, dtype=jnp.int32)
    angle = TWO_PI / count * (index[:, None] * index[None, :] % count).astype(jnp.float32)
    return (jnp.cos(angle), jnp.sin(angle))


def shards(
    density,
    stick_column,
    vloc,
    positions,
    species,
    psi,
    miller_wave,
    proj_radial,
    proj_count,
    dcoef,
    occupation,
):
    ga_index = lax.axis_index("ga")
    band_index = lax.axis_index("band")
    ga_count = lax.axis_size("ga")
    band_count = lax.axis_size("band")
    atom_count = positions.shape[1]
    kind_count = vloc.shape[0]
    slot_count = proj_radial.shape[1]
    sticks_here = vloc.shape[2]
    planes = density.shape[0]
    scale_norm = 1.0 / math.sqrt(NX * NY * NZ)
    start_zero = jnp.int32(0)
    cos_y, sin_y = dft_table(NY)
    cos_x, sin_x = dft_table(NX)
    batch_cos = jnp.broadcast_to(cos_x[None], (planes, NX, NX))
    batch_sin = jnp.broadcast_to(sin_x[None], (planes, NX, NX))
    xpass_real = jnp.einsum("pmx,pxy->pmy", batch_cos, density, precision=FINE).reshape(
        planes * NX, NY
    )
    xpass_imag = -jnp.einsum("pmx,pxy->pmy", batch_sin, density, precision=FINE).reshape(
        planes * NX, NY
    )
    full_real = jnp.dot(xpass_real, cos_y, precision=FINE) + jnp.dot(
        xpass_imag, sin_y, precision=FINE
    )
    full_imag = jnp.dot(xpass_imag, cos_y, precision=FINE) - jnp.dot(
        xpass_real, sin_y, precision=FINE
    )
    columns = jnp.concatenate(
        [full_real.reshape(planes, NX * NY), full_imag.reshape(planes, NX * NY)], axis=0
    )
    sub_sticks = sticks_here // band_count
    share_columns = lax.dynamic_slice_in_dim(
        stick_column.reshape(ga_count, band_count, sub_sticks), band_index, 1, 1
    ).reshape(ga_count * sub_sticks)
    picked_rows = jnp.take(columns.T, share_columns, axis=0)
    chosen = picked_rows.T.reshape(2 * planes, ga_count, sub_sticks).transpose(1, 0, 2)
    by_stick = lax.all_to_all(chosen, "ga", split_axis=0, concat_axis=0, tiled=True)
    by_stick = by_stick.reshape(ga_count * 2 * planes, sub_sticks)
    cos_z, sin_z = dft_table(NZ)
    cos_z = cos_z.reshape(NZ, ga_count, planes) * scale_norm
    sin_z = sin_z.reshape(NZ, ga_count, planes) * scale_norm
    table_z = jnp.stack(
        [jnp.stack([cos_z, sin_z], axis=2), jnp.stack([-sin_z, cos_z], axis=2)]
    ).reshape(2 * NZ, ga_count * 2 * planes)
    sub_values = jnp.dot(table_z, by_stick, precision=FINE).reshape(2, NZ, sub_sticks)
    density_sticks = lax.all_gather(sub_values, "band", axis=2, tiled=True)
    stick_start = ga_index * sticks_here + band_index * sub_sticks
    owned = lax.dynamic_slice_in_dim(stick_column, stick_start, sub_sticks)
    freq_x = frequency(owned // NY, NX).astype(jnp.float32)
    freq_y = frequency(owned % NY, NY).astype(jnp.float32)
    freq_z = frequency(jnp.arange(NZ, dtype=jnp.int32), NZ).astype(jnp.float32)
    wave_x = TWO_PI / NX * freq_x
    wave_y = TWO_PI / NY * freq_y
    wave_z = TWO_PI / NZ * freq_z
    angle_plane = TWO_PI * (
        positions[0][:, None] * freq_x[None, :] + positions[1][:, None] * freq_y[None, :]
    )
    angle_depth = TWO_PI * positions[2][:, None] * freq_z[None, :]
    plane_cos = jnp.cos(angle_plane)
    plane_sin = jnp.sin(angle_plane)
    plane_rows = jnp.stack(
        [
            plane_cos * wave_x[None, :],
            plane_cos * wave_y[None, :],
            plane_cos,
            plane_sin * wave_x[None, :],
            plane_sin * wave_y[None, :],
            plane_sin,
        ]
    ).reshape(6 * atom_count, sub_sticks)
    vloc_here = lax.dynamic_slice_in_dim(vloc, band_index * sub_sticks, sub_sticks, 2)
    fields = (vloc_here[:, None] * sub_values[None]).reshape(kind_count * 2 * NZ, sub_sticks)
    sums = lax.dot_general(plane_rows, fields, (((1,), (1,)), ((), ())), precision=FINE)
    sums = sums.reshape(2, 3, atom_count, kind_count, 2, NZ)
    all_pick = (species[:, None] == jnp.arange(kind_count, dtype=jnp.int32)[None, :]).astype(
        jnp.float32
    )
    sums = jnp.sum(sums * all_pick[None, None, :, :, None, None], axis=3)
    summed_real = sums[0, :, :, 0] - sums[1, :, :, 1]
    summed_imag = sums[0, :, :, 1] + sums[1, :, :, 0]
    depth_weight = jnp.stack([jnp.ones_like(wave_z), jnp.ones_like(wave_z), wave_z])
    local_part = jnp.sum(
        (jnp.cos(angle_depth)[None] * summed_imag + jnp.sin(angle_depth)[None] * summed_real)
        * depth_weight[:, None, :],
        axis=2,
    )
    bands_here = psi.shape[2]
    waves_here = psi.shape[0]
    psi_flat = psi.reshape(waves_here, 2 * bands_here)
    miller_f = miller_wave.astype(jnp.float32)
    weights = jnp.stack(
        [
            jnp.ones_like(miller_f[0]),
            TWO_PI / NX * miller_f[0],
            TWO_PI / NY * miller_f[1],
            TWO_PI / NZ * miller_f[2],
        ]
    )

    def project_block(block_start, block_rows):
        block_atoms = block_rows // slot_count
        atom_start = block_start // slot_count
        block_places = lax.dynamic_slice_in_dim(positions, atom_start, block_atoms, 1)
        block_kinds = lax.dynamic_slice_in_dim(species, atom_start, block_atoms)
        phase = TWO_PI * (
            block_places[0][:, None] * miller_f[0][None, :]
            + block_places[1][:, None] * miller_f[1][None, :]
            + block_places[2][:, None] * miller_f[2][None, :]
        )
        radial = jnp.zeros((block_atoms, slot_count, waves_here), jnp.float32)
        for kind_index in range(kind_count):
            match = (block_kinds == kind_index).astype(jnp.float32)
            radial = radial + match[:, None, None] * proj_radial[kind_index][None]
        parts = jnp.stack(
            [radial * jnp.cos(phase)[:, None, :], radial * jnp.sin(phase)[:, None, :]], axis=2
        )
        table = (parts[:, :, None] * weights[None, None, :, None, :]).astype(jnp.bfloat16)
        product = jnp.dot(
            table.reshape(block_rows * 8, waves_here), psi_flat, preferred_element_type=jnp.float32
        )
        product = product.reshape(block_rows, 4, 2, 2, bands_here)
        proj_real = product[:, :, 0, 0] - product[:, :, 1, 1]
        proj_imag = product[:, :, 0, 1] + product[:, :, 1, 0]
        return jnp.stack([proj_real, proj_imag], axis=2).reshape(block_rows, 8 * bands_here)

    share_rows = atom_count * slot_count // ga_count
    block_rows = 64
    starts = block_rows * jnp.arange(
        share_rows * lax.axis_size("ga") // block_rows, dtype=jnp.int32
    )

    def one_block(block_start):
        return project_block(block_start, block_rows)

    owned_rows = lax.psum_scatter(
        lax.map(one_block, starts).reshape(share_rows * lax.axis_size("ga"), 8 * bands_here),
        "ga",
        scatter_dimension=0,
        tiled=True,
    )
    per_ga = share_rows // slot_count
    ga_start = ga_index * per_ga
    terms = owned_rows.reshape(per_ga, slot_count, 4, 2, bands_here)
    ga_kinds = lax.dynamic_slice_in_dim(species, ga_start, per_ga)
    ga_pick = (ga_kinds[:, None] == jnp.arange(kind_count, dtype=jnp.int32)[None, :]).astype(
        jnp.float32
    )
    live_slots = (jnp.arange(slot_count, dtype=jnp.int32)[None, :] < proj_count[:, None]).astype(
        jnp.float32
    )
    kind_table = dcoef * live_slots[:, :, None] * live_slots[:, None, :]
    coupling = jnp.einsum("as,sij->aij", ga_pick, kind_table, precision=EXACT)
    mixed_real = jnp.einsum("aij,ajcn->aicn", coupling, terms[:, :, 1:, 0], precision=EXACT)
    mixed_imag = jnp.einsum("aij,ajcn->aicn", coupling, terms[:, :, 1:, 1], precision=EXACT)
    value = (
        terms[:, :, 0, 0][:, :, None, :] * mixed_imag
        - terms[:, :, 0, 1][:, :, None, :] * mixed_real
    )
    nonlocal_part = 2.0 * jnp.einsum("aicn,n->ca", value, occupation, precision=EXACT)
    nonlocal_full = lax.dynamic_update_slice(
        jnp.zeros((3, atom_count), jnp.float32), nonlocal_part, (start_zero, ga_start)
    )
    forces = lax.psum(local_part + nonlocal_full, ("band", "ga"))
    return (density_sticks, forces)


def solution(mesh):
    in_specs = (
        P("ga", None, None),
        P(),
        P(None, None, "ga"),
        P(),
        P(),
        P("ga", None, "band"),
        P(None, "ga"),
        P(None, None, "ga"),
        P(),
        P(),
        P("band"),
    )
    out_specs = (P(None, None, "ga"), P())
    return jax.shard_map(shards, mesh=mesh, in_specs=in_specs, out_specs=out_specs, check_vma=False)
```

profile of v0, /device:TPU:12, one launch (start us, length us, event | category | flops | bytes accessed | tf_op | source)
XLA Modules:
  0.0 485.3 jit_solution(1100664189729486365)
XLA Ops:
  12.0 83.8 %copy.56 = bf16[33792,2,256]{0,2,1:T(8,128)(2,1)} copy(bf16[33792,2,256]{2,1,0:T(2,128)(2,1)} %param.18) | data formatting | bytes 69206016 | tf_op args[5]
  98.0 206.9 %while.12 = (s32[]{:T(128)}, f32[4,64,2048]{2,1,0:T(8,128)}, s32[4]{0:T(128)}, s32[32]{0:T(128)S(1)}, f32[2,8,33792]{2,1,0:T(8,128)}, /*index=5*/f32[3,32]{1,0:T...) while((s32[]{:T(128)}, f32[4,64,2048]{2,1,0:T(8,128)}, ...), condition=%wide.region_3.4_spmd, body=%wide.region_2.3_spmd.sunk | while | flops 17768366080 | bytes 134012464 | solution.py:173
  103.8 5.2 %fusion.115 = (f32[8,33792]{1,0:T(8,128)}, f32[8,33792]{1,0:T(8,128)}) fusion(f32[33792]{0:T(1024)S(1)} %bitcast.204, f32[8]{0:T(128)S(1)} %get-tuple-element.244, f32[33792]{0:T(1024)S(1)} %bitcast.205, f32[8]{0:T(128)S(1)} %get-tuple-element.246, f32[33792]{0:T(1024)S(1)} %bitcast.203, f32[8]{0:T(128)S(1)} %get-tuple-element.248), kind=kLoop, calls=%fused_computation.14.clone.1 | loop fusion | flops 1622016 | bytes 2568288 | tf_op jit(solution)/shard_map/while/body/eval_jaxpr/cos | solution.py:152
  113.8 6.2 %pad_maximum_fusion.8 = f32[64,2,33792]{2,0,1:T(8,128)} fusion(f32[64,1,33792]{2,0,1:T(8,128)S(1)} %get-tuple-element.255, f32[64,1,33792]{2,0,1:T(8,128)S(1)} %get-tuple-element.256), kind=kLoop, calls=%fused_computation.6.clone.1 | loop fusion | flops 4325376 | bytes 34603008 | tf_op jit(solution)/shard_map/while/body/eval_jaxpr/stack | solution.py:151
  120.0 24.2 %fusion.116 = f32[64,4,2,2,256]{4,0,3,2,1:T(8,128)S(1)} fusion(bf16[2,256,33792,1,1]{2,1,0,4,3:T(8,128)(2,1)} %bitcast.198, f32[4,33792]{1,0:T(4,128)S(1)} %copy-done.5, f32[64,2,33792]{2,0,1:T(8,128)} %pad_maximum_fusion.8), kind=kOutput, calls=%fused_computation.3.clone.1 | convolution fusion | flops 17751343104 | bytes 53493760 | tf_op jit(solution)/shard_map/while/body/eval_jaxpr/dot_general | solution.py:155
  155.5 5.2 %fusion.115 = (f32[8,33792]{1,0:T(8,128)}, f32[8,33792]{1,0:T(8,128)}) fusion(f32[33792]{0:T(1024)S(1)} %bitcast.204, f32[8]{0:T(128)S(1)} %get-tuple-element.244, f32[33792]{0:T(1024)S(1)} %bitcast.205, f32[8]{0:T(128)S(1)} %get-tuple-element.246, f32[33792]{0:T(1024)S(1)} %bitcast.203, f32[8]{0:T(128)S(1)} %get-tuple-element.248), kind=kLoop, calls=%fused_computation.14.clone.1 | loop fusion | flops 1622016 | bytes 2568288 | tf_op jit(solution)/shard_map/while/body/eval_jaxpr/cos | solution.py:152
  165.5 6.2 %pad_maximum_fusion.8 = f32[64,2,33792]{2,0,1:T(8,128)} fusion(f32[64,1,33792]{2,0,1:T(8,128)S(1)} %get-tuple-element.255, f32[64,1,33792]{2,0,1:T(8,128)S(1)} %get-tuple-element.256), kind=kLoop, calls=%fused_computation.6.clone.1 | loop fusion | flops 4325376 | bytes 34603008 | tf_op jit(solution)/shard_map/while/body/eval_jaxpr/stack | solution.py:151
  171.7 24.2 %fusion.116 = f32[64,4,2,2,256]{4,0,3,2,1:T(8,128)S(1)} fusion(bf16[2,256,33792,1,1]{2,1,0,4,3:T(8,128)(2,1)} %bitcast.198, f32[4,33792]{1,0:T(4,128)S(1)} %copy-done.5, f32[64,2,33792]{2,0,1:T(8,128)} %pad_maximum_fusion.8), kind=kOutput, calls=%fused_computation.3.clone.1 | convolution fusion | flops 17751343104 | bytes 53493760 | tf_op jit(solution)/shard_map/while/body/eval_jaxpr/dot_general | solution.py:155
  207.2 5.2 %fusion.115 = (f32[8,33792]{1,0:T(8,128)}, f32[8,33792]{1,0:T(8,128)}) fusion(f32[33792]{0:T(1024)S(1)} %bitcast.204, f32[8]{0:T(128)S(1)} %get-tuple-element.244, f32[33792]{0:T(1024)S(1)} %bitcast.205, f32[8]{0:T(128)S(1)} %get-tuple-element.246, f32[33792]{0:T(1024)S(1)} %bitcast.203, f32[8]{0:T(128)S(1)} %get-tuple-element.248), kind=kLoop, calls=%fused_computation.14.clone.1 | loop fusion | flops 1622016 | bytes 2568288 | tf_op jit(solution)/shard_map/while/body/eval_jaxpr/cos | solution.py:152
  217.3 6.2 %pad_maximum_fusion.8 = f32[64,2,33792]{2,0,1:T(8,128)} fusion(f32[64,1,33792]{2,0,1:T(8,128)S(1)} %get-tuple-element.255, f32[64,1,33792]{2,0,1:T(8,128)S(1)} %get-tuple-element.256), kind=kLoop, calls=%fused_computation.6.clone.1 | loop fusion | flops 4325376 | bytes 34603008 | tf_op jit(solution)/shard_map/while/body/eval_jaxpr/stack | solution.py:151
  223.4 24.2 %fusion.116 = f32[64,4,2,2,256]{4,0,3,2,1:T(8,128)S(1)} fusion(bf16[2,256,33792,1,1]{2,1,0,4,3:T(8,128)(2,1)} %bitcast.198, f32[4,33792]{1,0:T(4,128)S(1)} %copy-done.5, f32[64,2,33792]{2,0,1:T(8,128)} %pad_maximum_fusion.8), kind=kOutput, calls=%fused_computation.3.clone.1 | convolution fusion | flops 17751343104 | bytes 53493760 | tf_op jit(solution)/shard_map/while/body/eval_jaxpr/dot_general | solution.py:155
  258.9 5.2 %fusion.115 = (f32[8,33792]{1,0:T(8,128)}, f32[8,33792]{1,0:T(8,128)}) fusion(f32[33792]{0:T(1024)S(1)} %bitcast.204, f32[8]{0:T(128)S(1)} %get-tuple-element.244, f32[33792]{0:T(1024)S(1)} %bitcast.205, f32[8]{0:T(128)S(1)} %get-tuple-element.246, f32[33792]{0:T(1024)S(1)} %bitcast.203, f32[8]{0:T(128)S(1)} %get-tuple-element.248), kind=kLoop, calls=%fused_computation.14.clone.1 | loop fusion | flops 1622016 | bytes 2568288 | tf_op jit(solution)/shard_map/while/body/eval_jaxpr/cos | solution.py:152
  269.0 6.2 %pad_maximum_fusion.8 = f32[64,2,33792]{2,0,1:T(8,128)} fusion(f32[64,1,33792]{2,0,1:T(8,128)S(1)} %get-tuple-element.255, f32[64,1,33792]{2,0,1:T(8,128)S(1)} %get-tuple-element.256), kind=kLoop, calls=%fused_computation.6.clone.1 | loop fusion | flops 4325376 | bytes 34603008 | tf_op jit(solution)/shard_map/while/body/eval_jaxpr/stack | solution.py:151
  275.1 24.2 %fusion.116 = f32[64,4,2,2,256]{4,0,3,2,1:T(8,128)S(1)} fusion(bf16[2,256,33792,1,1]{2,1,0,4,3:T(8,128)(2,1)} %bitcast.198, f32[4,33792]{1,0:T(4,128)S(1)} %copy-done.5, f32[64,2,33792]{2,0,1:T(8,128)} %pad_maximum_fusion.8), kind=kOutput, calls=%fused_computation.3.clone.1 | convolution fusion | flops 17751343104 | bytes 53493760 | tf_op jit(solution)/shard_map/while/body/eval_jaxpr/dot_general | solution.py:155
  307.7 2.5 fusion.15
  314.1 3.5 fusion.55
  317.6 3.6 convolution_add_fusion
  321.2 3.4 copy.50
  324.7 5.5 %reshape.1345 = f32[20,25600]{1,0:T(8,128)} reshape(f32[3200,160]{1,0:T(8,128)} %copy.50) | data formatting | bytes 4096000 | tf_op jit(solution)/shard_map/reshape | solution.py:66
  330.2 6.1 %convolution_subtract_fusion = f32[3200,160]{0,1:T(8,128)} fusion(f32[3200,160]{0,1:T(8,128)} %fusion.55, f32[3200,160]{1,0:T(8,128)} %bitcast.200), kind=kOutput, calls=%fused_computation.31 | convolution fusion | flops 492262400 | bytes 6144000 | tf_op jit(solution)/shard_map/dot_general | solution.py:62
  336.3 3.4 copy.51
  339.7 5.4 %reshape.1346 = f32[20,25600]{1,0:T(8,128)} reshape(f32[3200,160]{1,0:T(8,128)} %copy.51) | data formatting | bytes 4096000 | tf_op jit(solution)/shard_map/reshape | solution.py:66
  345.1 4.7 pad_maximum_fusion.2
  349.9 9.0 %copy.52 = f32[40,25600]{0,1:T(8,128)} copy(f32[40,25600]{1,0:T(8,128)} %pad_maximum_fusion.2) | data formatting | bytes 8192000 | tf_op jit(solution)/shard_map/concatenate | solution.py:65
  358.9 22.7 %gather_fusion = f32[5120,40]{1,0:T(8,128)} fusion(f32[25600,40]{1,0:T(8,128)} %bitcast.196, s32[5120]{0:T(1024)S(1)} %broadcast_clamp_fusion), kind=kCustom, calls=%fused_computation | custom fusion | bytes 1658880 | tf_op jit(solution)/shard_map/jit(_take)/gather | solution.py:72
  381.7 5.3 %broadcast_select_fusion = f32[5120,40]{1,0:T(8,128)} fusion(f32[5120,40]{1,0:T(8,128)} %gather_fusion, pred[5120]{0:T(1024)(128)(4,1)S(1)} %compare_and_fusion), kind=kLoop, calls=%fused_computation.41 | loop fusion | flops 204800 | bytes 1643520 | tf_op jit(solution)/shard_map/jit(_take)/select_n | solution.py:72
  386.9 2.8 copy.53
  389.8 6.3 %all-to-all-start = ((f32[8,40,640]{2,1,0:T(8,128)}), f32[8,40,640]{2,1,0:T(8,128)}, u32[]{:S(2)}, u32[]{:S(2)}) async-start(f32[8,40,640]{2,1,0:T(8,128)} %bitcast.207), calls=%async_computation | async-start | bytes 1638400 | tf_op jit(solution)/shard_map/all_to_all | solution.py:74
  404.4 10.9 %all-to-all-done = f32[8,40,640]{2,1,0:T(8,128)} async-done(((f32[8,40,640]{2,1,0:T(8,128)}), f32[8,40,640]{2,1,0:T(8,128)}, u32[]{:S(2)}, u32[]{:S(2)}) %all-to-all-start) | async-done | bytes 819232 | tf_op jit(solution)/shard_map/all_to_all | solution.py:74
  415.2 3.0 fusion.27
  432.1 41.9 %psum.7 = f32[3,32]{1,0:T(4,128)} all-reduce(f32[3,32]{1,0:T(4,128)} %add.270), channel_id=1, replica_groups=mesh['band'=4,'ga'=8] {'band','ga'}, use_global_device_ids=true, to_apply=%region_6.7 | all-reduce | flops 96 | bytes 768 | tf_op jit(solution)/shard_map/psum | solution.py:200
  474.0 3.9 copy.109
  (166 shorter events, 88.7 us)
Async XLA Ops:
  8.0 299.7 %copy-start = (f32[20,160,160]{2,1,0:T(8,128)S(1)}, f32[20,160,160]{2,1,0:T(8,128)}, u32[]{:S(2)}) copy-start(f32[20,160,160]{2,1,0:T(8,128)} %param.13) | copy-start | bytes 6144004
  8.0 418.9 %reduce-scatter.2.cloned.1.call-start = ((), (), s32[]{:S(2)}) async-start(), calls=%async_computation.3 | async-start | bytes 2359296 | tf_op jit(solution)/shard_map/reduce_scatter | solution.py:172
  10.1 0.8 copy-start.4
  12.0 86.0 %copy-start.6 = (f32[3,32]{1,0:T(4,128)S(1)}, f32[3,32]{1,0:T(4,128)}, u32[]{:S(2)}) copy-start(f32[3,32]{1,0:T(4,128)} %param.16) | copy-start | bytes 1156
  12.0 86.0 %copy-start.8 = (s32[32]{0:T(128)S(1)}, s32[32]{0:T(128)}, u32[]{:S(2)}) copy-start(s32[32]{0:T(128)} %param.17) | copy-start | bytes 388
  109.4 1.9 copy-start.1
  109.4 2.2 copy-start.2
  113.8 6.2 %copy-start.5 = (f32[4,33792]{1,0:T(4,128)S(1)}, f32[4,33792]{1,0:T(4,128)}, u32[]{:S(2)}) copy-start(f32[4,33792]{1,0:T(4,128)} %get-tuple-element.294) | copy-start | bytes 1622020 | tf_op jit(solution)/shard_map/while
  161.1 1.9 copy-start.1
  161.1 2.2 copy-start.2
  165.5 6.2 %copy-start.5 = (f32[4,33792]{1,0:T(4,128)S(1)}, f32[4,33792]{1,0:T(4,128)}, u32[]{:S(2)}) copy-start(f32[4,33792]{1,0:T(4,128)} %get-tuple-element.294) | copy-start | bytes 1622020 | tf_op jit(solution)/shard_map/while
  212.8 1.9 copy-start.1
  212.8 2.2 copy-start.2
  217.2 6.2 %copy-start.5 = (f32[4,33792]{1,0:T(4,128)S(1)}, f32[4,33792]{1,0:T(4,128)}, u32[]{:S(2)}) copy-start(f32[4,33792]{1,0:T(4,128)} %get-tuple-element.294) | copy-start | bytes 1622020 | tf_op jit(solution)/shard_map/while
  264.6 1.9 copy-start.1
  264.6 2.2 copy-start.2
  269.0 6.2 %copy-start.5 = (f32[4,33792]{1,0:T(4,128)S(1)}, f32[4,33792]{1,0:T(4,128)}, u32[]{:S(2)}) copy-start(f32[4,33792]{1,0:T(4,128)} %get-tuple-element.294) | copy-start | bytes 1622020 | tf_op jit(solution)/shard_map/while
  310.2 3.9 copy-start.3
  389.8 25.5 %all-to-all-start = ((f32[8,40,640]{2,1,0:T(8,128)}), f32[8,40,640]{2,1,0:T(8,128)}, u32[]{:S(2)}, u32[]{:S(2)}) async-start(f32[8,40,640]{2,1,0:T(8,128)} %bitcast.207), calls=%async_computation | async-start | bytes 1638400 | tf_op jit(solution)/shard_map/all_to_all | solution.py:74
  396.1 77.9 %all-gather.2.cloned.1.call-start = ((), (), s32[]{:S(2)}) async-start(), calls=%async_computation.2 | async-start | bytes 4096000 | tf_op jit(solution)/shard_map/all_gather | solution.py:83
  397.0 22.9 %copy-start.10 = (f32[2,8,8]{2,1,0:T(8,128)S(1)}, f32[2,8,8]{2,1,0:T(8,128)}, u32[]{:S(2)}) copy-start(f32[2,8,8]{2,1,0:T(8,128)} %param.22) | copy-start | bytes 1540
  399.7 21.8 %copy-start.9 = (s32[32]{0:T(128)S(1)}, s32[32]{0:T(128)}, u32[]{:S(2)}) copy-start(s32[32]{0:T(128)} %param.17) | copy-start | bytes 388
  399.7 21.8 %copy-start.7 = (f32[3,32]{1,0:T(4,128)S(1)}, f32[3,32]{1,0:T(4,128)}, u32[]{:S(2)}) copy-start(f32[3,32]{1,0:T(4,128)} %param.16) | copy-start | bytes 1156
Sparse Core Ops, SparseCore 0:
  305.0 68.7 reduce-scatter.1
Sparse Core Ops, SparseCore 1:
  418.4 29.1 all-gather.1
where the time goes:
time: 489 us; the launch traced here: 485 us
  local copies, waits for them, and re-layouts  197 us (40%)
  matrix products  123 us (25%)
  other arithmetic  79.5 us (16%)
  blocking collectives  41.9 us (9%)
  between operations  15.8 us (3%)
  waiting for transfers between devices  10.9 us (2%)
  loops' own time  10.7 us (2%)
  starting transfers between devices  6.33 us (1%)
    dot_general x4, matrix products, project_block(): jnp.dot(table.reshape(block_rows * 8, waves_here), psi_flat, preferred_el...  96.8 us
    unnamed x19, local copies, waits for them, and re-layouts  88.5 us
    psum x1, blocking collectives, shards(): forces = lax.psum(local_part + nonlocal_full, ('band', 'ga'))  41.9 us
    another operation x4, other arithmetic, project_block(): jnp.stack([radial * jnp.cos(phase)[:, None, :], radial * jnp.sin(phase)[:...  24.7 us
    gather x1, local copies, waits for them, and re-layouts, shards(): picked_rows = jnp.take(columns.T, share_columns, axis=0)  22.7 us
    cos x4, other arithmetic, project_block(): jnp.cos(phase)[:, None, :]  20.9 us
    all_to_all x1, waiting for transfers between devices, shards(): lax.all_to_all(chosen, 'ga', split_axis=0, concat_axis=0, tiled=True)  10.9 us
    another operation x1, loops' own time, shards(): lax.map(one_block, starts)  10.7 us
  transfers between devices with their start and end apart: 3, of which 1 were waited for; matrix products, arithmetic and copies ran while one was open for 23% of the time, Pallas kernels for 0%

commit v1 on v0

--- a/solution.py
+++ b/solution.py
@@ -197,7 +197,9 @@
     nonlocal_full = lax.dynamic_update_slice(
         jnp.zeros((3, atom_count), jnp.float32), nonlocal_part, (start_zero, ga_start)
     )
-    forces = lax.psum(local_part + nonlocal_full, ("band", "ga"))
+    part = local_part + nonlocal_full
+    pieces = lax.all_gather(part, ("band", "ga"), axis=0, tiled=False)
+    forces = pieces.sum(axis=0)
     return (density_sticks, forces)
 
 

time: 489 us -> 518 us (1.059); the launches traced: 485 us -> 508 us
  blocking collectives: 41.9 us -> 64.3 us
    all_gather x0 -> x1, blocking collectives: none -> 64.3 us  [shards(): pieces = lax.all_gather(part, ('band', 'ga'), axis=0, tiled=False)]
    psum x1 -> x0, blocking collectives: 41.9 us -> none  [shards(): forces = lax.psum(local_part + nonlocal_full, ('band', 'ga'))]
  transfers between devices with their start and end apart: 3 -> 3, of which waited for: 1 -> 1; matrix products, arithmetic and copies ran while one was open for 23% -> 22% of each run, Pallas kernels for 0% -> 0%
where the time goes in v1:
time: 518 us; the launch traced here: 508 us
  local copies, waits for them, and re-layouts  197 us (38%)
  matrix products  123 us (24%)
  other arithmetic  80.1 us (15%)
  blocking collectives  64.3 us (12%)
  between operations  15.8 us (3%)
  waiting for transfers between devices  10.9 us (2%)
  loops' own time  10.7 us (2%)
  starting transfers between devices  6.33 us (1%)
    dot_general x4, matrix products, project_block(): jnp.dot(table.reshape(block_rows * 8, waves_here), psi_flat, preferred_el...  96.8 us
    unnamed x19, local copies, waits for them, and re-layouts  88.5 us
    all_gather x1, blocking collectives, shards(): pieces = lax.all_gather(part, ('band', 'ga'), axis=0, tiled=False)  64.3 us
    another operation x4, other arithmetic, project_block(): jnp.stack([radial * jnp.cos(phase)[:, None, :], radial * jnp.sin(phase)[:...  24.7 us
    gather x1, local copies, waits for them, and re-layouts, shards(): picked_rows = jnp.take(columns.T, share_columns, axis=0)  22.7 us
    cos x4, other arithmetic, project_block(): jnp.cos(phase)[:, None, :]  20.9 us
    all_to_all x1, waiting for transfers between devices, shards(): lax.all_to_all(chosen, 'ga', split_axis=0, concat_axis=0, tiled=True)  10.9 us
    another operation x1, loops' own time, shards(): lax.map(one_block, starts)  10.7 us
  transfers between devices with their start and end apart: 3, of which 1 were waited for; matrix products, arithmetic and copies ran while one was open for 22% of the time, Pallas kernels for 0%

profile of v1, /device:TPU:12, one launch (start us, length us, event | category | flops | bytes accessed | tf_op | source)
XLA Modules:
  0.0 508.4 jit_solution(16990386369384040606)
XLA Ops:
  12.0 83.8 %copy.56 = bf16[33792,2,256]{0,2,1:T(8,128)(2,1)} copy(bf16[33792,2,256]{2,1,0:T(2,128)(2,1)} %param.18) | data formatting | bytes 69206016 | tf_op args[5]
  98.0 206.9 %while.12 = (s32[]{:T(128)}, f32[4,64,2048]{2,1,0:T(8,128)}, s32[4]{0:T(128)}, s32[32]{0:T(128)S(1)}, f32[2,8,33792]{2,1,0:T(8,128)}, /*index=5*/f32[3,32]{1,0:T...) while((s32[]{:T(128)}, f32[4,64,2048]{2,1,0:T(8,128)}, ...), condition=%wide.region_3.4_spmd, body=%wide.region_2.3_spmd.sunk | while | flops 17768366080 | bytes 134012464 | solution.py:173
  103.8 5.2 %fusion.116 = (f32[8,33792]{1,0:T(8,128)}, f32[8,33792]{1,0:T(8,128)}) fusion(f32[33792]{0:T(1024)S(1)} %bitcast.209, f32[8]{0:T(128)S(1)} %get-tuple-element.244, f32[33792]{0:T(1024)S(1)} %bitcast.210, f32[8]{0:T(128)S(1)} %get-tuple-element.246, f32[33792]{0:T(1024)S(1)} %bitcast.208, f32[8]{0:T(128)S(1)} %get-tuple-element.248), kind=kLoop, calls=%fused_computation.14.clone.1 | loop fusion | flops 1622016 | bytes 2568288 | tf_op jit(solution)/shard_map/while/body/eval_jaxpr/cos | solution.py:152
  113.8 6.2 %pad_maximum_fusion.8 = f32[64,2,33792]{2,0,1:T(8,128)} fusion(f32[64,1,33792]{2,0,1:T(8,128)S(1)} %get-tuple-element.255, f32[64,1,33792]{2,0,1:T(8,128)S(1)} %get-tuple-element.256), kind=kLoop, calls=%fused_computation.6.clone.1 | loop fusion | flops 4325376 | bytes 34603008 | tf_op jit(solution)/shard_map/while/body/eval_jaxpr/stack | solution.py:151
  120.0 24.2 %fusion.117 = f32[64,4,2,2,256]{4,0,3,2,1:T(8,128)S(1)} fusion(bf16[2,256,33792,1,1]{2,1,0,4,3:T(8,128)(2,1)} %bitcast.203, f32[4,33792]{1,0:T(4,128)S(1)} %copy-done.5, f32[64,2,33792]{2,0,1:T(8,128)} %pad_maximum_fusion.8), kind=kOutput, calls=%fused_computation.3.clone.1 | convolution fusion | flops 17751343104 | bytes 53493760 | tf_op jit(solution)/shard_map/while/body/eval_jaxpr/dot_general | solution.py:155
  155.5 5.2 %fusion.116 = (f32[8,33792]{1,0:T(8,128)}, f32[8,33792]{1,0:T(8,128)}) fusion(f32[33792]{0:T(1024)S(1)} %bitcast.209, f32[8]{0:T(128)S(1)} %get-tuple-element.244, f32[33792]{0:T(1024)S(1)} %bitcast.210, f32[8]{0:T(128)S(1)} %get-tuple-element.246, f32[33792]{0:T(1024)S(1)} %bitcast.208, f32[8]{0:T(128)S(1)} %get-tuple-element.248), kind=kLoop, calls=%fused_computation.14.clone.1 | loop fusion | flops 1622016 | bytes 2568288 | tf_op jit(solution)/shard_map/while/body/eval_jaxpr/cos | solution.py:152
  165.5 6.2 %pad_maximum_fusion.8 = f32[64,2,33792]{2,0,1:T(8,128)} fusion(f32[64,1,33792]{2,0,1:T(8,128)S(1)} %get-tuple-element.255, f32[64,1,33792]{2,0,1:T(8,128)S(1)} %get-tuple-element.256), kind=kLoop, calls=%fused_computation.6.clone.1 | loop fusion | flops 4325376 | bytes 34603008 | tf_op jit(solution)/shard_map/while/body/eval_jaxpr/stack | solution.py:151
  171.7 24.2 %fusion.117 = f32[64,4,2,2,256]{4,0,3,2,1:T(8,128)S(1)} fusion(bf16[2,256,33792,1,1]{2,1,0,4,3:T(8,128)(2,1)} %bitcast.203, f32[4,33792]{1,0:T(4,128)S(1)} %copy-done.5, f32[64,2,33792]{2,0,1:T(8,128)} %pad_maximum_fusion.8), kind=kOutput, calls=%fused_computation.3.clone.1 | convolution fusion | flops 17751343104 | bytes 53493760 | tf_op jit(solution)/shard_map/while/body/eval_jaxpr/dot_general | solution.py:155
  207.2 5.2 %fusion.116 = (f32[8,33792]{1,0:T(8,128)}, f32[8,33792]{1,0:T(8,128)}) fusion(f32[33792]{0:T(1024)S(1)} %bitcast.209, f32[8]{0:T(128)S(1)} %get-tuple-element.244, f32[33792]{0:T(1024)S(1)} %bitcast.210, f32[8]{0:T(128)S(1)} %get-tuple-element.246, f32[33792]{0:T(1024)S(1)} %bitcast.208, f32[8]{0:T(128)S(1)} %get-tuple-element.248), kind=kLoop, calls=%fused_computation.14.clone.1 | loop fusion | flops 1622016 | bytes 2568288 | tf_op jit(solution)/shard_map/while/body/eval_jaxpr/cos | solution.py:152
  217.3 6.2 %pad_maximum_fusion.8 = f32[64,2,33792]{2,0,1:T(8,128)} fusion(f32[64,1,33792]{2,0,1:T(8,128)S(1)} %get-tuple-element.255, f32[64,1,33792]{2,0,1:T(8,128)S(1)} %get-tuple-element.256), kind=kLoop, calls=%fused_computation.6.clone.1 | loop fusion | flops 4325376 | bytes 34603008 | tf_op jit(solution)/shard_map/while/body/eval_jaxpr/stack | solution.py:151
  223.4 24.2 %fusion.117 = f32[64,4,2,2,256]{4,0,3,2,1:T(8,128)S(1)} fusion(bf16[2,256,33792,1,1]{2,1,0,4,3:T(8,128)(2,1)} %bitcast.203, f32[4,33792]{1,0:T(4,128)S(1)} %copy-done.5, f32[64,2,33792]{2,0,1:T(8,128)} %pad_maximum_fusion.8), kind=kOutput, calls=%fused_computation.3.clone.1 | convolution fusion | flops 17751343104 | bytes 53493760 | tf_op jit(solution)/shard_map/while/body/eval_jaxpr/dot_general | solution.py:155
  258.9 5.2 %fusion.116 = (f32[8,33792]{1,0:T(8,128)}, f32[8,33792]{1,0:T(8,128)}) fusion(f32[33792]{0:T(1024)S(1)} %bitcast.209, f32[8]{0:T(128)S(1)} %get-tuple-element.244, f32[33792]{0:T(1024)S(1)} %bitcast.210, f32[8]{0:T(128)S(1)} %get-tuple-element.246, f32[33792]{0:T(1024)S(1)} %bitcast.208, f32[8]{0:T(128)S(1)} %get-tuple-element.248), kind=kLoop, calls=%fused_computation.14.clone.1 | loop fusion | flops 1622016 | bytes 2568288 | tf_op jit(solution)/shard_map/while/body/eval_jaxpr/cos | solution.py:152
  269.0 6.2 %pad_maximum_fusion.8 = f32[64,2,33792]{2,0,1:T(8,128)} fusion(f32[64,1,33792]{2,0,1:T(8,128)S(1)} %get-tuple-element.255, f32[64,1,33792]{2,0,1:T(8,128)S(1)} %get-tuple-element.256), kind=kLoop, calls=%fused_computation.6.clone.1 | loop fusion | flops 4325376 | bytes 34603008 | tf_op jit(solution)/shard_map/while/body/eval_jaxpr/stack | solution.py:151
  275.1 24.2 %fusion.117 = f32[64,4,2,2,256]{4,0,3,2,1:T(8,128)S(1)} fusion(bf16[2,256,33792,1,1]{2,1,0,4,3:T(8,128)(2,1)} %bitcast.203, f32[4,33792]{1,0:T(4,128)S(1)} %copy-done.5, f32[64,2,33792]{2,0,1:T(8,128)} %pad_maximum_fusion.8), kind=kOutput, calls=%fused_computation.3.clone.1 | convolution fusion | flops 17751343104 | bytes 53493760 | tf_op jit(solution)/shard_map/while/body/eval_jaxpr/dot_general | solution.py:155
  307.7 2.5 fusion.15
  314.1 3.5 fusion.55
  317.6 3.6 convolution_add_fusion
  321.2 3.4 copy.50
  324.7 5.5 %reshape.1347 = f32[20,25600]{1,0:T(8,128)} reshape(f32[3200,160]{1,0:T(8,128)} %copy.50) | data formatting | bytes 4096000 | tf_op jit(solution)/shard_map/reshape | solution.py:66
  330.2 6.1 %convolution_subtract_fusion = f32[3200,160]{0,1:T(8,128)} fusion(f32[3200,160]{0,1:T(8,128)} %fusion.55, f32[3200,160]{1,0:T(8,128)} %bitcast.205), kind=kOutput, calls=%fused_computation.31 | convolution fusion | flops 492262400 | bytes 6144000 | tf_op jit(solution)/shard_map/dot_general | solution.py:62
  336.3 3.4 copy.51
  339.7 5.4 %reshape.1348 = f32[20,25600]{1,0:T(8,128)} reshape(f32[3200,160]{1,0:T(8,128)} %copy.51) | data formatting | bytes 4096000 | tf_op jit(solution)/shard_map/reshape | solution.py:66
  345.1 4.7 pad_maximum_fusion.2
  349.9 9.0 %copy.52 = f32[40,25600]{0,1:T(8,128)} copy(f32[40,25600]{1,0:T(8,128)} %pad_maximum_fusion.2) | data formatting | bytes 8192000 | tf_op jit(solution)/shard_map/concatenate | solution.py:65
  358.9 22.7 %gather_fusion = f32[5120,40]{1,0:T(8,128)} fusion(f32[25600,40]{1,0:T(8,128)} %bitcast.201, s32[5120]{0:T(1024)S(1)} %broadcast_clamp_fusion), kind=kCustom, calls=%fused_computation | custom fusion | bytes 1658880 | tf_op jit(solution)/shard_map/jit(_take)/gather | solution.py:72
  381.7 5.3 %broadcast_select_fusion = f32[5120,40]{1,0:T(8,128)} fusion(f32[5120,40]{1,0:T(8,128)} %gather_fusion, pred[5120]{0:T(1024)(128)(4,1)S(1)} %compare_and_fusion), kind=kLoop, calls=%fused_computation.41 | loop fusion | flops 204800 | bytes 1643520 | tf_op jit(solution)/shard_map/jit(_take)/select_n | solution.py:72
  386.9 2.8 copy.53
  389.8 6.3 %all-to-all-start = ((f32[8,40,640]{2,1,0:T(8,128)}), f32[8,40,640]{2,1,0:T(8,128)}, u32[]{:S(2)}, u32[]{:S(2)}) async-start(f32[8,40,640]{2,1,0:T(8,128)} %bitcast.212), calls=%async_computation | async-start | bytes 1638400 | tf_op jit(solution)/shard_map/all_to_all | solution.py:74
  404.4 10.9 %all-to-all-done = f32[8,40,640]{2,1,0:T(8,128)} async-done(((f32[8,40,640]{2,1,0:T(8,128)}), f32[8,40,640]{2,1,0:T(8,128)}, u32[]{:S(2)}, u32[]{:S(2)}) %all-to-all-start) | async-done | bytes 819232 | tf_op jit(solution)/shard_map/all_to_all | solution.py:74
  415.2 3.0 fusion.27
  432.1 64.3 %all_gather.14 = f32[32,3,32]{2,1,0:T(4,128)S(1)} all-gather(f32[1,3,32]{2,1,0:T(4,128)} %add.268), channel_id=1, replica_groups=mesh['band'=4,'ga'=8] {'band','ga'}, dimensions={0}, use_global_device_ids=true | all-gather | bytes 12672 | tf_op jit(solution)/shard_map/all_gather | solution.py:201
  497.1 3.9 copy.109
  (167 shorter events, 89.3 us)
Async XLA Ops:
  8.0 299.7 %copy-start = (f32[20,160,160]{2,1,0:T(8,128)S(1)}, f32[20,160,160]{2,1,0:T(8,128)}, u32[]{:S(2)}) copy-start(f32[20,160,160]{2,1,0:T(8,128)} %param.13) | copy-start | bytes 6144004
  8.0 418.9 %reduce-scatter.2.cloned.1.call-start = ((), (), s32[]{:S(2)}) async-start(), calls=%async_computation.3 | async-start | bytes 2359296 | tf_op jit(solution)/shard_map/reduce_scatter | solution.py:172
  10.1 0.8 copy-start.4
  12.0 86.0 %copy-start.6 = (f32[3,32]{1,0:T(4,128)S(1)}, f32[3,32]{1,0:T(4,128)}, u32[]{:S(2)}) copy-start(f32[3,32]{1,0:T(4,128)} %param.16) | copy-start | bytes 1156
  12.0 86.0 %copy-start.8 = (s32[32]{0:T(128)S(1)}, s32[32]{0:T(128)}, u32[]{:S(2)}) copy-start(s32[32]{0:T(128)} %param.17) | copy-start | bytes 388
  109.4 1.9 copy-start.1
  109.4 2.2 copy-start.2
  113.8 6.2 %copy-start.5 = (f32[4,33792]{1,0:T(4,128)S(1)}, f32[4,33792]{1,0:T(4,128)}, u32[]{:S(2)}) copy-start(f32[4,33792]{1,0:T(4,128)} %get-tuple-element.294) | copy-start | bytes 1622020 | tf_op jit(solution)/shard_map/while
  161.1 1.9 copy-start.1
  161.1 2.2 copy-start.2
  165.5 6.2 %copy-start.5 = (f32[4,33792]{1,0:T(4,128)S(1)}, f32[4,33792]{1,0:T(4,128)}, u32[]{:S(2)}) copy-start(f32[4,33792]{1,0:T(4,128)} %get-tuple-element.294) | copy-start | bytes 1622020 | tf_op jit(solution)/shard_map/while
  212.8 1.9 copy-start.1
  212.8 2.2 copy-start.2
  217.2 6.2 %copy-start.5 = (f32[4,33792]{1,0:T(4,128)S(1)}, f32[4,33792]{1,0:T(4,128)}, u32[]{:S(2)}) copy-start(f32[4,33792]{1,0:T(4,128)} %get-tuple-element.294) | copy-start | bytes 1622020 | tf_op jit(solution)/shard_map/while
  264.6 1.9 copy-start.1
  264.6 2.2 copy-start.2
  269.0 6.2 %copy-start.5 = (f32[4,33792]{1,0:T(4,128)S(1)}, f32[4,33792]{1,0:T(4,128)}, u32[]{:S(2)}) copy-start(f32[4,33792]{1,0:T(4,128)} %get-tuple-element.294) | copy-start | bytes 1622020 | tf_op jit(solution)/shard_map/while
  310.2 3.9 copy-start.3
  389.8 25.5 %all-to-all-start = ((f32[8,40,640]{2,1,0:T(8,128)}), f32[8,40,640]{2,1,0:T(8,128)}, u32[]{:S(2)}, u32[]{:S(2)}) async-start(f32[8,40,640]{2,1,0:T(8,128)} %bitcast.212), calls=%async_computation | async-start | bytes 1638400 | tf_op jit(solution)/shard_map/all_to_all | solution.py:74
  396.1 101.0 %all-gather.2.cloned.1.call-start = ((), (), s32[]{:S(2)}) async-start(), calls=%async_computation.2 | async-start | bytes 4096000 | tf_op jit(solution)/shard_map/all_gather | solution.py:83
  397.0 22.9 %copy-start.10 = (f32[2,8,8]{2,1,0:T(8,128)S(1)}, f32[2,8,8]{2,1,0:T(8,128)}, u32[]{:S(2)}) copy-start(f32[2,8,8]{2,1,0:T(8,128)} %param.22) | copy-start | bytes 1540
  399.7 21.8 %copy-start.9 = (s32[32]{0:T(128)S(1)}, s32[32]{0:T(128)}, u32[]{:S(2)}) copy-start(s32[32]{0:T(128)} %param.17) | copy-start | bytes 388
  399.7 21.8 %copy-start.7 = (f32[3,32]{1,0:T(4,128)S(1)}, f32[3,32]{1,0:T(4,128)}, u32[]{:S(2)}) copy-start(f32[3,32]{1,0:T(4,128)} %param.16) | copy-start | bytes 1156
Sparse Core Ops, SparseCore 0:
  305.0 68.7 reduce-scatter.1
Sparse Core Ops, SparseCore 1:
  418.4 28.5 all-gather.1
